TPU v7x, 32 devices: a whole 2x2x4 slice. The times are simulated.
32 devices in a mesh: row: 4 (over z), col: 8 (over y, x, core).
Axes of the slice: x: 2, y: 2, z: 4, core: 2. Of those that a mesh axis runs over, the one named last changes fastest.
Arguments:
- frames: float32 [512, 64, 1024], P(('row', 'col')), may hold values from -1 to 6
- class_index: int32 [64, 1024], P('row', 'col'), may hold values from 0 to 7
- surface_mask: int32 [64, 1024], P('row', 'col'), may hold values 0 or 1
- effusivity: float32 [8], replicated, may hold values from 0.5 to 2
- conductivity: float32 [8], replicated, may hold values from 0.2 to 1
Outputs:
- heat_flux: float32 [64, 1024, 512], P('row', 'col')
All inputs are finite; a program needn't handle non-finite values. No bound on the sum of `surface_mask` on one device may be relied on, other than what follows from the above.
Results may differ from a plain program's by a relative error of at most 0.0003.
Values sent between devices are 32-bit elements; how exact they have to be, the bound alone decides.
A program may use at most 64 MiB of HBM per device.

v0:
```python
import functools
import jax
import jax.numpy as jnp
from jax import lax
from jax.experimental import pallas as pl
from jax.experimental.pallas import tpu as pltpu
from jax.sharding import PartitionSpec as P

PASSES = 3
PAD = 8
GROUP = 8
LANES = 128
VMEM_GATHER = 40 * 2**20
MESH = pl.DeviceIdType.MESH

flux_factor = 1.1283791670955126
lateral_rate = 0.24


def extended(block, sides, width):
    for axis, dim in sides:
        count = lax.axis_size(axis)
        forward = [(i, i + 1) for i in range(count - 1)]
        backward = [(target, source) for source, target in forward]
        low = lax.ppermute(
            lax.slice_in_dim(block, block.shape[dim] - width, None, axis=dim), axis, forward
        )
        high = lax.ppermute(lax.slice_in_dim(block, 0, width, axis=dim), axis, backward)
        block = jnp.concatenate([low, block, high], axis=dim)
    return block


def weights(lagged):
    clipped = jnp.maximum(lagged, 0.0)
    return jnp.where(lagged >= 0.0, 1.0 / (jnp.sqrt(clipped) + jnp.sqrt(clipped + 1.0)), 0.0)


def kernel_from(later, earlier):
    lagged = (later[:, None] - earlier[None, :]).astype(jnp.float32)
    return weights(lagged) - weights(lagged - 1.0)


def relax_once(padded, lateral):
    center = padded[1:-1, 1:-1]
    laplace = (
        padded[2:, 1:-1] + padded[:-2, 1:-1] + padded[1:-1, 2:] + padded[1:-1, :-2] - 4.0 * center
    )
    return center + lateral[:, :, None] * laplace


def plain_device(frames, class_index, surface_mask, effusivity, conductivity):
    row_count = lax.axis_size("row")
    col_count = lax.axis_size("col")
    local_frames, height, width = frames.shape
    tile_rows = height // row_count
    tile_cols = width // col_count
    total_frames = local_frames * row_count * col_count
    frame_ids = jnp.arange(total_frames, dtype=jnp.int32)
    contract = (((0,), (1,)), ((), ()))
    kernel = kernel_from(frame_ids, frame_ids)
    blocks = frames.reshape(local_frames, row_count, tile_rows, col_count, tile_cols)
    blocks = blocks.transpose(0, 1, 3, 2, 4).reshape(
        local_frames, row_count * col_count, tile_rows, tile_cols
    )
    convolved = lax.dot_general(
        lax.all_to_all(blocks, ("row", "col"), split_axis=1, concat_axis=0, tiled=True)[:, 0],
        kernel,
        contract,
        precision=lax.Precision.HIGHEST,
    )
    classes = jnp.arange(effusivity.shape[0], dtype=jnp.int32)
    matches = (class_index[:, :, None] == classes[None, None, :]).astype(jnp.float32)
    maskf = surface_mask.astype(jnp.float32)
    gain = flux_factor * jnp.sum(matches * effusivity, axis=-1) * maskf
    lateral = lateral_rate * jnp.sum(matches * conductivity, axis=-1) * maskf
    heat_flux = convolved * gain[:, :, None]
    padded = extended(heat_flux, (("row", 0), ("col", 1)), PASSES)
    lateral_wide = extended(lateral, (("row", 0), ("col", 1)), PASSES - 1)
    for pass_index in range(PASSES):
        margin = PASSES - 1 - pass_index
        offset = PASSES - 1 - margin
        lateral_part = lateral_wide[
            offset : offset + tile_rows + 2 * margin, offset : offset + tile_cols + 2 * margin
        ]
        padded = relax_once(padded, lateral_part)
    return padded


SIDES = ((-1, 0), (1, 0), (0, -1), (0, 1), (-1, -1), (-1, 1), (1, -1), (1, 1))


def gather_kernel(
    rows, cols, tile_rows, tile_cols, local,
    frames, class_ref, mask_ref, eff_ref, cond_ref,
    flux, wide,
    held, lat, near, gain, mix_ref, edge, rim, strip, side_out, side_in,
    send_sem, recv_sem, own_sem, lat_send, lat_recv,
    strip_send, strip_recv, strip_own, relay_send, relay_recv, side_send, side_recv,
):
    row, col = lax.axis_index("row"), lax.axis_index("col")
    group = cols * local
    total = rows * group
    halo = PASSES
    chunks = total // LANES
    mid = rows // 2
    half = row // mid

    def there(step, count, at):
        return (at + step >= 0) & (at + step < count)

    def exists(side):
        return there(side[0], rows, row) & there(side[1], cols, col)

    classes = class_ref[...]
    maskf = mask_ref[...].astype(jnp.float32)
    eff = jnp.zeros(classes.shape, jnp.float32)
    cond = jnp.zeros(classes.shape, jnp.float32)
    for k in range(eff_ref.shape[0]):
        eff = jnp.where(classes == k, eff_ref[k], eff)
        cond = jnp.where(classes == k, cond_ref[k], cond)
    gain_rows = flux_factor * eff * maskf
    lat_rows = lateral_rate * cond * maskf
    lat[0] = lat_rows
    lat[1] = gain_rows
    near[...] = jnp.zeros_like(near)

    @pl.loop(0, tile_rows + 2 * halo)
    def _(h):
        for c in range(chunks):
            flux[c, h] = jnp.zeros(flux.shape[2:], jnp.float32)

    barrier = pltpu.get_barrier_semaphore()
    for k in range(rows):
        @pl.loop(0 if k else 1, cols)
        def _(j, k=k):
            pl.semaphore_signal(
                barrier, inc=1,
                device_id=(lax.rem(row + k, rows), lax.rem(col + j, cols)),
                device_id_type=MESH,
            )
    pl.semaphore_wait(barrier, rows * cols - 1)

    def lat_copy(i):
        side = SIDES[i]
        return pltpu.make_async_remote_copy(
            src_ref=lat, dst_ref=near.at[i], send_sem=lat_send.at[i], recv_sem=lat_recv.at[i],
            device_id=(row + side[0], col + side[1]), device_id_type=MESH,
        )

    def column(at):
        return pl.ds(pl.multiple_of(at * tile_cols, tile_cols), tile_cols)

    own = pltpu.make_async_copy(
        frames.at[:, pl.ds(pl.multiple_of(row * tile_rows, tile_rows), tile_rows), column(col)],
        held.at[pl.ds((row * cols + col) * local, local)],
        own_sem,
    )
    own.start()

    strip_row = mid - 1 + half
    strip_from = pl.ds(pl.multiple_of(mid * tile_rows - GROUP * half, GROUP), GROUP)
    strip_at = strip.at[pl.ds(((row - half * mid) * cols + col) * local, local)]
    beside = row == strip_row

    def strip_copy(j):
        to_col = lax.rem(col + j, cols)
        return pltpu.make_async_remote_copy(
            src_ref=frames.at[:, strip_from, column(to_col)], dst_ref=strip_at,
            send_sem=strip_send, recv_sem=strip_recv.at[row - half * mid],
            device_id=(strip_row, to_col), device_id_type=MESH,
        )

    strip_self = pltpu.make_async_copy(frames.at[:, strip_from, column(col)], strip_at, strip_own)

    def start_strips():
        @pl.loop(1, cols)
        def _(j):
            strip_copy(j).start()

        @pl.when(beside)
        def _():
            strip_self.start()

        @pl.when(jnp.logical_not(beside))
        def _():
            strip_copy(0).start()

    order = [mid, 0] + [k for k in range(1, rows) if k != mid]
    for k in order:
        @pl.loop(0 if k else 1, cols)
        def _(j, k=k):
            to_row, to_col = lax.rem(row + k, rows), lax.rem(col + j, cols)
            pltpu.make_async_remote_copy(
                src_ref=frames.at[
                    :, pl.ds(pl.multiple_of(to_row * tile_rows, tile_rows), tile_rows), column(to_col)
                ],
                dst_ref=held.at[pl.ds((row * cols + col) * local, local)],
                send_sem=send_sem, recv_sem=recv_sem.at[k],
                device_id=(to_row, to_col), device_id_type=MESH,
            ).start()
        if k == 0:
            start_strips()
        if k == order[0]:
            for i, side in enumerate(SIDES):
                @pl.when(exists(side))
                def _(i=i):
                    lat_copy(i).start()
    for k in range(rows):
        shape = (group, total)
        earlier = lax.broadcasted_iota(jnp.int32, shape, 0) + k * group
        later = lax.broadcasted_iota(jnp.int32, shape, 1)
        lagged = (later - earlier).astype(jnp.float32)
        mix = weights(lagged) - weights(lagged - 1.0)
        high = mix.astype(jnp.bfloat16)
        mix_ref[0, k * group : (k + 1) * group] = high
        mix_ref[1, k * group : (k + 1) * group] = (mix - high.astype(jnp.float32)).astype(jnp.bfloat16)

    def upright(line):
        return jnp.transpose(jnp.broadcast_to(line, (tile_cols, tile_cols)))[:, :LANES]

    for i, side in enumerate(SIDES):
        @pl.when(exists((-side[0], -side[1])))
        def _(i=i):
            lat_copy(i).wait_recv()
        @pl.when(exists(side))
        def _(i=i):
            lat_copy(i).wait_send()
    slot = {(-a, -b): i for i, (a, b) in enumerate(SIDES)}
    inside = slice(PAD, PAD + tile_cols)
    for h in range(-halo, tile_rows + halo):
        up = -1 if h < 0 else (1 if h >= tile_rows else 0)
        at = h - up * tile_rows
        def line(side, which=0):
            if side == (0, 0):
                return lat[which, at : at + 1, :]
            return near[slot[side], which, at : at + 1, :]
        wide[h + halo, inside] = upright(line((up, 0)))
        wide[h + halo, 0:PAD] = upright(line((up, -1)))[tile_cols - PAD :]
        wide[h + halo, PAD + tile_cols :] = upright(line((up, 1)))[:PAD]
        gain[h + halo] = upright(line((up, 0), 1))

    def frames_of(source):
        return pl.ds(pl.multiple_of(source * group, group), group)

    def product(x, source):
        count = x.shape[0]
        x = jnp.transpose(x, (0, 2, 1)).reshape(count * tile_cols, group)
        high = x.astype(jnp.bfloat16)
        low = (x - high.astype(jnp.float32)).astype(jnp.bfloat16)
        at = frames_of(source)
        out = jnp.dot(high, mix_ref[0, at], preferred_element_type=jnp.float32)
        out += jnp.dot(low, mix_ref[0, at], preferred_element_type=jnp.float32)
        out += jnp.dot(high, mix_ref[1, at], preferred_element_type=jnp.float32)
        return out.reshape(count, tile_cols, total)

    def wait_for(ref, sem):
        pltpu.make_async_copy(ref, ref, sem).wait()

    def relayed(side, at_row, source):
        if side == 0:
            return (at_row >= 1) & jnp.logical_not((at_row == mid) & (source < mid))
        return (at_row < rows - 1) & jnp.logical_not((at_row == mid - 1) & (source >= mid))

    def relay_copy(side, k):
        source = lax.rem(row - k + rows, rows)
        at = frames_of(source)
        return pltpu.make_async_remote_copy(
            src_ref=edge.at[side, :, at], dst_ref=rim.at[1 - side, :, at],
            send_sem=relay_send.at[side, k], recv_sem=relay_recv.at[1 - side, k],
            device_id=(row + (1 if side else -1), col), device_id_type=MESH,
        )

    def add(here, out, finish):
        for c in range(chunks):
            value = flux[c, here, inside] + out[:, :, c * LANES : (c + 1) * LANES]
            flux[c, here, inside] = value * gain[here] if finish else value

    last = tile_rows // GROUP - 1

    def main_part(k, finish):
        source = lax.rem(row - k + rows, rows)
        if k == 0:
            own.wait()
            wait_for(held.at[pl.ds(0, group - local)], recv_sem.at[k])
        else:
            wait_for(held.at[pl.ds(0, group)], recv_sem.at[k])
        at = frames_of(source)
        for q in range(last + 1):
            x = jnp.swapaxes(held[at, q * GROUP : (q + 1) * GROUP, :], 0, 1)
            if q == 0:
                edge[0, :, at] = x[:halo]
            if q == last:
                edge[1, :, at] = x[GROUP - halo :]
        for side in range(2):
            @pl.when(relayed(side, row, source))
            def _(side=side):
                relay_copy(side, k).start()
        for q in range(last + 1):
            x = jnp.swapaxes(held[at, q * GROUP : (q + 1) * GROUP, :], 0, 1)
            here = slice(halo + q * GROUP, halo + (q + 1) * GROUP)
            add(here, product(x, source), finish)

    def halo_part(k, finish):
        for side in range(2):
            beyond = row + (1 if side else -1)
            source = lax.rem(beyond - k + rows, rows)
            at = frames_of(source)
            here = slice(halo + tile_rows, 2 * halo + tile_rows) if side else slice(0, halo)

            @pl.when(there(1 if side else -1, rows, row))
            def _(side=side, beyond=beyond, source=source, at=at, here=here):
                direct = jnp.logical_not(relayed(1 - side, beyond, source))

                @pl.when(direct)
                def _():
                    turn = source - half * mid

                    @pl.when(source == row)
                    def _():
                        strip_self.wait()
                        wait_for(strip.at[pl.ds(0, group - local)], strip_recv.at[turn])

                    @pl.when(source != row)
                    def _():
                        wait_for(strip.at[pl.ds(0, group)], strip_recv.at[turn])

                    x = jnp.swapaxes(strip[frames_of(turn)], 0, 1)
                    rim[side, :, at] = x[:halo] if side else x[GROUP - halo :]

                @pl.when(jnp.logical_not(direct))
                def _():
                    wait_for(rim.at[side, :, at], relay_recv.at[side, k])

                add(here, product(rim[side, :, at], source), finish)

    visits = order
    for k in visits[:-1]:
        main_part(k, False)
    for k in visits[:-2]:
        halo_part(k, False)
    main_part(visits[-1], True)
    halo_part(visits[-2], False)
    halo_part(visits[-1], True)

    def side_copy(i):
        return pltpu.make_async_remote_copy(
            src_ref=side_out.at[i], dst_ref=side_in.at[1 - i],
            send_sem=side_send.at[i], recv_sem=side_recv.at[1 - i],
            device_id=(row, col + (1 if i else -1)), device_id_type=MESH,
        )

    for i in range(2):
        for j in range(halo):
            at = PAD + j + (tile_cols - halo if i else 0)
            for c in range(chunks):
                side_out[i, j, c] = flux[c, :, at, :]
    for i in range(2):
        @pl.when(there(1 if i else -1, cols, col))
        def _(i=i):
            side_copy(i).start()

    wait_for(held.at[pl.ds(0, total - local)], send_sem)

    @pl.when(beside)
    def _():
        wait_for(strip.at[pl.ds(0, group - local)], strip_send)

    @pl.when(jnp.logical_not(beside))
    def _():
        wait_for(strip.at[pl.ds(0, group)], strip_send)

    for k in range(rows):
        for side in range(2):
            @pl.when(relayed(side, row, lax.rem(row - k + rows, rows)))
            def _(side=side, k=k):
                relay_copy(side, k).wait_send()
    for i in range(2):
        @pl.when(there(1 if i else -1, cols, col))
        def _(i=i):
            side_copy(i).wait_send()
            wait_for(side_in.at[i], side_recv.at[i])
            for j in range(halo):
                at = PAD + tile_cols + j if i else PAD - halo + j
                for c in range(chunks):
                    flux[c, :, at, :] = side_in[i, j, c]


def relax_kernel(flux, wide, out, first, second, third, sem):
    chunks, count, width = flux.shape[0], flux.shape[1], flux.shape[2]

    def out_copy(c):
        return pltpu.make_async_copy(
            third.at[c], out.at[:, :, c * LANES : (c + 1) * LANES], sem.at[c]
        )

    for c in range(chunks):
        source = flux.at[c]
        for step, target in enumerate((first, second, None)):
            if target is None:
                bounds = [PAD, PAD + (width - 2 * PAD) // 2, width - PAD]
            else:
                bounds = [1 + step, width // 2, width - 1 - step]
            for a, b in zip(bounds[:-1], bounds[1:]):
                above, center = source[step, a:b, :], source[step + 1, a:b, :]
                for h in range(step + 1, count - step - 1):
                    below = source[h + 1, a:b, :]
                    laplace = (
                        below + above
                        + source[h, a + 1 : b + 1, :] + source[h, a - 1 : b - 1, :] - 4.0 * center
                    )
                    value = center + wide[h, a:b, :] * laplace
                    if target is None:
                        third[c, h - PASSES, a - PAD : b - PAD] = value
                    else:
                        target[h, a:b, :] = value
                    above, center = center, below
            source = target
        out_copy(c).start()
    for c in range(chunks):
        out_copy(c).wait()


def per_device(frames, class_index, surface_mask, effusivity, conductivity):
    rows = lax.axis_size("row")
    cols = lax.axis_size("col")
    local, height, width = frames.shape
    tile_rows, tile_cols = height // rows, width // cols
    total = local * rows * cols
    if rows % 2 or local % 8 or tile_rows % GROUP or tile_cols != LANES or total % LANES or (local * cols) % LANES:
        return plain_device(frames, class_index, surface_mask, effusivity, conductivity)
    chunks = total // LANES
    high_rows, wide_cols = tile_rows + 2 * PASSES, tile_cols + 2 * PAD
    vmem = pl.BlockSpec(memory_space=pltpu.VMEM)
    smem = pl.BlockSpec(memory_space=pltpu.SMEM)
    dma = pltpu.SemaphoreType.DMA
    sides = len(SIDES)
    arguments = (frames, class_index, surface_mask, effusivity, conductivity)
    flux, wide = pl.pallas_call(
        functools.partial(gather_kernel, rows, cols, tile_rows, tile_cols, local),
        out_shape=(
            jax.ShapeDtypeStruct((chunks, high_rows, wide_cols, LANES), jnp.float32),
            jax.ShapeDtypeStruct((high_rows, wide_cols, LANES), jnp.float32),
        ),
        in_specs=[pl.BlockSpec(memory_space=pltpu.HBM), vmem, vmem, smem, smem],
        out_specs=(vmem, vmem),
        scratch_shapes=[
            pltpu.VMEM((total, tile_rows, tile_cols), jnp.float32),
            pltpu.VMEM((2, tile_rows, tile_cols), jnp.float32),
            pltpu.VMEM((sides, 2, tile_rows, tile_cols), jnp.float32),
            pltpu.VMEM((high_rows, tile_cols, LANES), jnp.float32),
            pltpu.VMEM((2, total, total), jnp.bfloat16),
            pltpu.VMEM((2, PASSES, total, tile_cols), jnp.float32),
            pltpu.VMEM((2, PASSES, total, tile_cols), jnp.float32),
            pltpu.VMEM((total // 2, GROUP, tile_cols), jnp.float32),
            pltpu.VMEM((2, PASSES, chunks, high_rows, LANES), jnp.float32),
            pltpu.VMEM((2, PASSES, chunks, high_rows, LANES), jnp.float32),
            dma, dma((rows,)), dma, dma((sides,)), dma((sides,)),
            dma, dma((rows // 2,)), dma, dma((2, rows)), dma((2, rows)), dma((2,)), dma((2,)),
        ],
        compiler_params=pltpu.CompilerParams(
            collective_id=0, has_side_effects=True, vmem_limit_bytes=VMEM_GATHER
        ),
        name="gather",
    )(*(pltpu.with_memory_space_constraint(x, pltpu.HBM) for x in arguments))
    return pl.pallas_call(
        relax_kernel,
        out_shape=jax.ShapeDtypeStruct((tile_rows, tile_cols, total), jnp.float32),
        in_specs=[vmem, vmem],
        out_specs=pl.BlockSpec(memory_space=pltpu.HBM),
        scratch_shapes=[pltpu.VMEM((high_rows, wide_cols, LANES), jnp.float32)] * 2
        + [pltpu.VMEM((chunks, tile_rows, tile_cols, LANES), jnp.float32), dma((chunks,))],
        compiler_params=pltpu.CompilerParams(vmem_limit_bytes=24 * 2**20),
        name="relax",
    )(flux, wide)


def solution(mesh):
    in_specs = (P(("row", "col"), None, None), P("row", "col"), P("row", "col"), P(), P())
    out_specs = P("row", "col", None)
    return jax.shard_map(
        per_device, mesh=mesh, in_specs=in_specs, out_specs=out_specs, check_vma=False
    )
```

profile of v0, /device:TPU:0, one launch (start us, length us, event | category | flops | bytes accessed | tf_op | source)
XLA Modules:
  0.0 118.6 jit_solution(17021822981523047896)
XLA Ops:
  0.0 113.9 %gather.1 = (f32[4,22,144,128]{3,2,1,0:T(8,128)S(1)}, f32[22,144,128]{2,1,0:T(8,128)S(1)}) custom-call(f32[16,64,1024]{2,1,0:T(8,128)} %frames.1, s32[16,128]{1,0:T(8,128)} %class_ref.1, s32[16,128]{1,0:T(8,128)} %mask_ref.1, f32[8]{0:T(128)} %eff_ref.1, f32[8]{0:T(128)} %cond_ref.1), custom_call_target="tpu_custom_call" | custom-call | tf_op jit(solution)/shard_map/gather/pallas_call | solution.py:438
  113.9 4.6 %relax.1 = f32[16,128,512]{2,1,0:T(8,128)} custom-call(f32[4,22,144,128]{3,2,1,0:T(8,128)S(1)} %get-tuple-element.7.flux, f32[22,144,128]{2,1,0:T(8,128)S(1)} %get-tuple-element.8.wide), custom_call_target="tpu_custom_call" | custom-call | tf_op jit(solution)/shard_map/relax/pallas_call | solution.py:465
where the time goes:
time: 121 us; the launch traced here: 119 us
  Pallas kernels  118 us (98%)
    pallas_call x1, Pallas kernels, per_device(): pl.pallas_call(functools.partial(gather_kernel, rows, cols, tile_rows, ti...  114 us
    pallas_call x1, Pallas kernels, per_device(): pl.pallas_call(relax_kernel, out_shape=jax.ShapeDtypeStruct((tile_rows, t...  4.57 us

commit v1 on v0

v1 whole, which is shorter than its diff:
```python
import functools
import jax
import jax.numpy as jnp
from jax import lax
from jax.experimental import pallas as pl
from jax.experimental.pallas import tpu as pltpu
from jax.sharding import PartitionSpec as P

PASSES = 3
PAD = 8
GROUP = 8
LANES = 128
STEPS = 8
VMEM_GATHER = 40 * 2**20
MESH = pl.DeviceIdType.MESH

flux_factor = 1.1283791670955126
lateral_rate = 0.24


def extended(block, sides, width):
    for axis, dim in sides:
        count = lax.axis_size(axis)
        forward = [(i, i + 1) for i in range(count - 1)]
        backward = [(target, source) for source, target in forward]
        low = lax.ppermute(
            lax.slice_in_dim(block, block.shape[dim] - width, None, axis=dim), axis, forward
        )
        high = lax.ppermute(lax.slice_in_dim(block, 0, width, axis=dim), axis, backward)
        block = jnp.concatenate([low, block, high], axis=dim)
    return block


def weights(lagged):
    clipped = jnp.maximum(lagged, 0.0)
    return jnp.where(lagged >= 0.0, 1.0 / (jnp.sqrt(clipped) + jnp.sqrt(clipped + 1.0)), 0.0)


def kernel_from(later, earlier):
    lagged = (later[:, None] - earlier[None, :]).astype(jnp.float32)
    return weights(lagged) - weights(lagged - 1.0)


def relax_once(padded, lateral):
    center = padded[1:-1, 1:-1]
    laplace = (
        padded[2:, 1:-1] + padded[:-2, 1:-1] + padded[1:-1, 2:] + padded[1:-1, :-2] - 4.0 * center
    )
    return center + lateral[:, :, None] * laplace


def plain_device(frames, class_index, surface_mask, effusivity, conductivity):
    row_count = lax.axis_size("row")
    col_count = lax.axis_size("col")
    local_frames, height, width = frames.shape
    tile_rows = height // row_count
    tile_cols = width // col_count
    total_frames = local_frames * row_count * col_count
    frame_ids = jnp.arange(total_frames, dtype=jnp.int32)
    contract = (((0,), (1,)), ((), ()))
    kernel = kernel_from(frame_ids, frame_ids)
    blocks = frames.reshape(local_frames, row_count, tile_rows, col_count, tile_cols)
    blocks = blocks.transpose(0, 1, 3, 2, 4).reshape(
        local_frames, row_count * col_count, tile_rows, tile_cols
    )
    convolved = lax.dot_general(
        lax.all_to_all(blocks, ("row", "col"), split_axis=1, concat_axis=0, tiled=True)[:, 0],
        kernel,
        contract,
        precision=lax.Precision.HIGHEST,
    )
    classes = jnp.arange(effusivity.shape[0], dtype=jnp.int32)
    matches = (class_index[:, :, None] == classes[None, None, :]).astype(jnp.float32)
    maskf = surface_mask.astype(jnp.float32)
    gain = flux_factor * jnp.sum(matches * effusivity, axis=-1) * maskf
    lateral = lateral_rate * jnp.sum(matches * conductivity, axis=-1) * maskf
    heat_flux = convolved * gain[:, :, None]
    padded = extended(heat_flux, (("row", 0), ("col", 1)), PASSES)
    lateral_wide = extended(lateral, (("row", 0), ("col", 1)), PASSES - 1)
    for pass_index in range(PASSES):
        margin = PASSES - 1 - pass_index
        offset = PASSES - 1 - margin
        lateral_part = lateral_wide[
            offset : offset + tile_rows + 2 * margin, offset : offset + tile_cols + 2 * margin
        ]
        padded = relax_once(padded, lateral_part)
    return padded


def gather_kernel(
    rows, cols, tile_rows, tile_cols, local, height, steps,
    frames, class_in, mask_in, eff_in, cond_in,
    held, flux, mix_ref,
    x, coef, done, done_far, first, second, edge_out, edge_in,
    class_ref, mask_ref, eff_ref, cond_ref,
    load_sem, small_sem, coef_send, near_recv, pair_recv, far_recv,
    raw_send, raw_recv, edge_send, edge_recv,
    near_send, cross_send, relay_send, recv_sem,
):
    row, col = lax.axis_index("row"), lax.axis_index("col")
    mid = rows // 2
    half = row // mid
    other = 1 - half
    half_rows = height // 2
    total = rows * cols * local
    halo = PASSES
    near = mid * cols - 1
    part = tile_rows // steps
    source = row * cols + col
    mirror, pair = rows - 1 - row, lax.rem(row + mid, rows)
    raw = ((row == mid - 1) | (row == mid)) & (lax.rem(col, 2) == 0)

    def wait_for(ref, sem):
        pltpu.make_async_copy(ref, ref, sem).wait()

    def aligned(value, unit):
        return pl.multiple_of(value, unit)

    def remote(src, dst, send, recv, to_row, to_col):
        return pltpu.make_async_remote_copy(
            src_ref=src, dst_ref=dst, send_sem=send, recv_sem=recv,
            device_id=(to_row, to_col), device_id_type=MESH,
        )

    def in_half(i):
        at = lax.rem(row * cols + col - half * (near + 1) + i, near + 1)
        return half * mid + at // cols, lax.rem(at, cols)

    smalls = [
        pltpu.make_async_copy(src, dst, small_sem.at[i])
        for i, (src, dst) in enumerate(
            ((class_in, class_ref), (mask_in, mask_ref), (eff_in, eff_ref), (cond_in, cond_ref))
        )
    ]
    for copy in smalls:
        copy.start()
    for c in range(cols):
        pltpu.make_async_copy(
            frames.at[:, :, c * LANES : (c + 1) * LANES], x.at[c, 0:local], load_sem
        ).start()

    barrier = pltpu.get_barrier_semaphore()

    @pl.when(raw)
    def _():
        pl.semaphore_signal(barrier, inc=1, device_id=(mirror, col), device_id_type=MESH)

    pl.semaphore_signal(barrier, inc=1, device_id=(pair, col), device_id_type=MESH)

    @pl.loop(1, near + 1)
    def _(i):
        pl.semaphore_signal(barrier, inc=1, device_id=in_half(i), device_id_type=MESH)

    for copy in smalls:
        copy.wait()
    classes = class_ref[...]
    maskf = mask_ref[...].astype(jnp.float32)
    eff = jnp.zeros(classes.shape, jnp.float32)
    cond = jnp.zeros(classes.shape, jnp.float32)
    for k in range(eff_ref.shape[0]):
        eff = jnp.where(classes == k, eff_ref[k], eff)
        cond = jnp.where(classes == k, cond_ref[k], cond)

    def tile_of(at_row, at_col):
        return coef.at[at_col, :, pl.ds(aligned(PAD + at_row * tile_rows, PAD), tile_rows)]

    own_rows = pl.ds(aligned(PAD + row * tile_rows, PAD), tile_rows)
    coef[col, 0, own_rows] = lateral_rate * cond * maskf
    coef[col, 1, own_rows] = flux_factor * eff * maskf
    for c in range(cols):
        for k in range(2):
            coef[c, k, 0:PAD] = jnp.zeros((PAD, LANES), jnp.float32)
            coef[c, k, PAD + height : 2 * PAD + height] = jnp.zeros((PAD, LANES), jnp.float32)

    pl.semaphore_wait(barrier, near + 1 + raw.astype(jnp.int32))

    own_tile, pair_tile = tile_of(row, col), tile_of(pair, col)
    remote(own_tile, own_tile, coef_send.at[0], pair_recv, pair, col).start()

    @pl.loop(1, near + 1)
    def _(i):
        to_row, to_col = in_half(i)
        remote(own_tile, own_tile, coef_send.at[1], near_recv, to_row, to_col).start()

    far_rows = pl.ds(aligned(other * half_rows, PAD), half_rows)
    near_rows = pl.ds(aligned(half * half_rows, PAD), half_rows)

    def raw_copy(c):
        return remote(
            frames.at[0:GROUP, far_rows, c * LANES : (c + 1) * LANES],
            x.at[c, local : local + GROUP, far_rows],
            raw_send, raw_recv, mirror, col,
        )

    edge_copy = remote(edge_out, edge_in, edge_send, edge_recv, mirror, col)

    @pl.when(raw)
    def _():
        for c in range(cols):
            raw_copy(c).start()

    wait_for(x.at[:, 0:local], load_sem)
    lines = x.reshape(cols, (local + GROUP) * height, LANES)

    def line(c, group, at):
        return lines[c, pl.ds(group * (GROUP * height) + at, GROUP, stride=height), :]

    @pl.when(raw)
    def _():
        for k in range(halo):
            for c in range(cols):
                edge_out[k, c] = line(c, 0, half_rows - halo * other + k)
        edge_copy.start()

    def fill_mix():
        block = tile_cols

        @pl.loop(0, total // block)
        def _(k):
            shape = (block, total)
            earlier = lax.broadcasted_iota(jnp.int32, shape, 0) + k * block
            later = lax.broadcasted_iota(jnp.int32, shape, 1)
            lagged = (later - earlier).astype(jnp.float32)
            mix = weights(lagged) - weights(lagged - 1.0)
            high = mix.astype(jnp.bfloat16)
            at = pl.ds(aligned(k * block, block), block)
            mix_ref[0, at] = high
            mix_ref[1, at] = (mix - high.astype(jnp.float32)).astype(jnp.bfloat16)

    lane = lax.broadcasted_iota(jnp.int32, (GROUP, LANES), 1)
    leftmost, rightmost = lane == 0, lane == LANES - 1
    nothing = jnp.zeros((GROUP, LANES), jnp.float32)

    def spread(c, which, at):
        return coef[c, which, pl.ds(at, GROUP, stride=0), :]

    def clear(side):
        for k in range(halo):
            for c in range(cols):
                first[(half_rows + halo) * side + k, c] = nothing

    def relax(source_ref, side, begin, end, store):
        base = side * half_rows - halo + PAD

        @pl.loop(begin, end)
        def _(i):
            center = [source_ref[i, c] for c in range(cols)]
            ahead = [pltpu.roll(v, 1, 1) for v in center]
            behind = [pltpu.roll(v, LANES - 1, 1) for v in center]
            for c in range(cols):
                left = jnp.where(leftmost, ahead[c - 1] if c else nothing, ahead[c])
                right = jnp.where(rightmost, behind[c + 1] if c + 1 < cols else nothing, behind[c])
                laplace = source_ref[i + 1, c] + source_ref[i - 1, c] + right + left - 4.0 * center[c]
                store(i, c, center[c] + spread(c, 0, base + i) * laplace)

    def passes(side, store_last):
        def keep(ref):
            def store(i, c, value):
                ref[i, c] = value
            return store

        span = half_rows + 2 * halo
        relax(first, side, 1, span - 1, keep(second))
        relax(second, side, 2, span - 2, keep(first))
        relax(first, side, halo, span - halo, store_last)

    def sweep(side, group):
        clear(side)

        @pl.loop(0, half_rows + halo)
        def _(k):
            at = (half_rows - halo) * side + k
            for c in range(cols):
                first[halo * (1 - side) + k, c] = spread(c, 1, at + PAD) * line(c, group, at)

        def store(i, c, value):
            j = i - halo
            at = pl.ds(aligned(group * GROUP, GROUP), GROUP)
            done[side * mid + j // tile_rows, c, lax.rem(j, tile_rows), at, :] = value

        passes(side, store)

    def sweep_raw():
        clear(half)

        @pl.loop(0, half_rows)
        def _(k):
            at = half_rows * half + k
            for c in range(cols):
                first[halo + k, c] = spread(c, 1, at + PAD) * line(c, local // GROUP, at)

        for k in range(halo):
            for c in range(cols):
                at = half_rows - halo * half + k
                first[(half_rows + halo) * (1 - half) + k, c] = spread(c, 1, at + PAD) * edge_in[k, c]

        def store(i, c, value):
            j = i - halo
            done_far[j // tile_rows, c, lax.rem(j, tile_rows), :, :] = value

        passes(half, store)

    groups = local // GROUP

    def rows_of(q):
        return pl.ds(q * part, part)

    def slots(at, count):
        return pl.ds(aligned(at, GROUP), count)

    fill_mix()

    wait_for(pair_tile, pair_recv)

    @pl.loop(1, near + 1)
    def _(i):
        to_row, to_col = in_half(i)
        remote(pair_tile, pair_tile, coef_send.at[2], far_recv, to_row, to_col).start()

    def tiles(count):
        return held.at[pl.ds(0, count), pl.ds(0, 2 * tile_rows)]

    wait_for(tiles(near), near_recv)
    wait_for(tiles(near), far_recv)

    @pl.loop(0, groups)
    def _(g):
        sweep(half, g)

    own_slots = slots(source * local, local)

    def near_copy(q, i):
        to_row, to_col = in_half(i)
        return remote(
            done.at[to_row, to_col, rows_of(q)], held.at[rows_of(q), own_slots],
            near_send, recv_sem.at[q], to_row, to_col,
        )

    @pl.loop(0, steps)
    def _(q):
        pltpu.make_async_copy(
            done.at[row, col, rows_of(q)], held.at[rows_of(q), own_slots], recv_sem.at[q]
        ).start()

        @pl.loop(1, near + 1)
        def _(i):
            near_copy(q, i).start()

    @pl.loop(raw.astype(jnp.int32), groups)
    def _(g):
        sweep(other, g)

    def across(i):
        at = lax.rem(row * cols + col - half * (near + 1) + i, near + 1)
        return other * mid + at // cols, lax.rem(at, cols)

    def start_cross(skip):
        count = local - skip

        @pl.loop(0, steps)
        def _(q):
            @pl.loop(0, near + 1)
            def _(i):
                to_row, to_col = across(i)
                remote(
                    done.at[to_row, to_col, rows_of(q), pl.ds(skip, count)],
                    held.at[rows_of(q), slots(source * local + skip, count)],
                    cross_send, recv_sem.at[q], to_row, to_col,
                ).start()

    @pl.when(raw)
    def _():
        start_cross(GROUP)

    @pl.when(jnp.logical_not(raw))
    def _():
        start_cross(0)

    @pl.when(raw)
    def _():
        wait_for(x.at[:, local : local + GROUP, near_rows], raw_recv)
        edge_copy.wait_recv()
        sweep_raw()
        there = slots((mirror * cols + col) * local, GROUP)

        @pl.loop(0, steps)
        def _(q):
            pltpu.make_async_copy(
                done_far.at[row - half * mid, col, rows_of(q)], held.at[rows_of(q), there],
                recv_sem.at[q],
            ).start()

            @pl.loop(1, near + 1)
            def _(i):
                to_row, to_col = in_half(i)
                remote(
                    done_far.at[to_row - half * mid, to_col, rows_of(q)],
                    held.at[rows_of(q), there],
                    relay_send, recv_sem.at[q], to_row, to_col,
                ).start()

    @pl.loop(0, steps - 1)
    def _(q):
        wait_for(held.at[rows_of(q)], recv_sem.at[q])
        convolve(held, mix_ref, flux, q * part, part)

    wait_for(held.at[rows_of(steps - 1)], recv_sem.at[steps - 1])

    wait_for(own_tile, coef_send.at[0])
    wait_for(tiles(near), coef_send.at[1])
    wait_for(tiles(near), coef_send.at[2])
    wait_for(held.at[:, pl.ds(0, near * local)], near_send)

    @pl.when(raw)
    def _():
        wait_for(x.at[:, local : local + GROUP, far_rows], raw_send)
        edge_copy.wait_send()
        wait_for(held.at[:, pl.ds(0, (near + 1) * (local - GROUP))], cross_send)
        wait_for(held.at[:, pl.ds(0, near * GROUP)], relay_send)

    @pl.when(jnp.logical_not(raw))
    def _():
        wait_for(held.at[:, pl.ds(0, (near + 1) * local)], cross_send)


def convolve(held, mix_ref, flux, begin, count):
    total, width = held.shape[1], held.shape[2]
    x = jnp.transpose(held[pl.ds(begin, count)], (0, 2, 1)).reshape(count * width, total)
    high = x.astype(jnp.bfloat16)
    low = (x - high.astype(jnp.float32)).astype(jnp.bfloat16)
    cut = total // 2
    for a, b in ((0, cut), (cut, total)):
        out = jnp.dot(high[:, :b], mix_ref[0, :b, a:b], preferred_element_type=jnp.float32)
        out += jnp.dot(low[:, :b], mix_ref[0, :b, a:b], preferred_element_type=jnp.float32)
        out += jnp.dot(high[:, :b], mix_ref[1, :b, a:b], preferred_element_type=jnp.float32)
        flux[pl.ds(begin, count), :, a:b] = out.reshape(count, width, b - a)


def finish_kernel(part, held, flux, mix_ref, out, last, sem):
    rows = held.shape[0]
    ready = rows - part
    early = pltpu.make_async_copy(flux.at[0:ready], out.at[0:ready], sem.at[0])
    early.start()
    convolve(held.at[ready:rows], mix_ref, last, 0, part)
    late = pltpu.make_async_copy(last, out.at[ready:rows], sem.at[1])
    late.start()
    early.wait()
    late.wait()


def per_device(frames, class_index, surface_mask, effusivity, conductivity):
    rows = lax.axis_size("row")
    cols = lax.axis_size("col")
    local, height, width = frames.shape
    tile_rows, tile_cols = height // rows, width // cols
    total = local * rows * cols
    near = rows // 2 * cols - 1
    fits = (
        rows % 2 == 0 and cols % 2 == 0 and local % (2 * GROUP) == 0 and tile_rows % PAD == 0
        and tile_rows % STEPS == 0 and tile_cols == LANES and total % (2 * LANES) == 0
        and near <= tile_rows and 2 * tile_rows <= total
    )
    if not fits:
        return plain_device(frames, class_index, surface_mask, effusivity, conductivity)
    half_rows, span = height // 2, height // 2 + 2 * PASSES
    vmem = pl.BlockSpec(memory_space=pltpu.VMEM)
    hbm = pl.BlockSpec(memory_space=pltpu.HBM)
    dma = pltpu.SemaphoreType.DMA
    f32 = jnp.float32
    arguments = (frames, class_index, surface_mask, effusivity, conductivity)
    held, flux, mix = pl.pallas_call(
        functools.partial(gather_kernel, rows, cols, tile_rows, tile_cols, local, height, STEPS),
        out_shape=(
            jax.ShapeDtypeStruct((tile_rows, total, LANES), f32),
            jax.ShapeDtypeStruct((tile_rows, tile_cols, total), f32),
            jax.ShapeDtypeStruct((2, total, total), jnp.bfloat16),
        ),
        in_specs=[hbm] * 5,
        out_specs=(vmem, vmem, vmem),
        scratch_shapes=[
            pltpu.VMEM((cols, local + GROUP, height, LANES), f32),
            pltpu.VMEM((cols, 2, height + 2 * PAD, LANES), f32),
            pltpu.VMEM((rows, cols, tile_rows, local, LANES), f32),
            pltpu.VMEM((rows // 2, cols, tile_rows, GROUP, LANES), f32),
            pltpu.VMEM((span, cols, GROUP, LANES), f32),
            pltpu.VMEM((span, cols, GROUP, LANES), f32),
            pltpu.VMEM((PASSES, cols, GROUP, LANES), f32),
            pltpu.VMEM((PASSES, cols, GROUP, LANES), f32),
            pltpu.VMEM((tile_rows, tile_cols), jnp.int32),
            pltpu.VMEM((tile_rows, tile_cols), jnp.int32),
            pltpu.SMEM(effusivity.shape, f32),
            pltpu.SMEM(conductivity.shape, f32),
            dma, dma((4,)), dma((3,)), dma, dma, dma,
            dma, dma, dma, dma,
            dma, dma, dma, dma((STEPS,)),
        ],
        compiler_params=pltpu.CompilerParams(
            collective_id=0, has_side_effects=True, vmem_limit_bytes=VMEM_GATHER
        ),
        name="gather",
    )(*(pltpu.with_memory_space_constraint(a, pltpu.HBM) for a in arguments))
    part = tile_rows // STEPS
    return pl.pallas_call(
        functools.partial(finish_kernel, part),
        out_shape=jax.ShapeDtypeStruct((tile_rows, tile_cols, total), f32),
        in_specs=[vmem, vmem, vmem],
        out_specs=hbm,
        scratch_shapes=[pltpu.VMEM((part, tile_cols, total), f32), dma((2,))],
        compiler_params=pltpu.CompilerParams(vmem_limit_bytes=24 * 2**20),
        name="finish",
    )(held, flux, mix)


def solution(mesh):
    in_specs = (P(("row", "col"), None, None), P("row", "col"), P("row", "col"), P(), P())
    out_specs = P("row", "col", None)
    return jax.shard_map(
        per_device, mesh=mesh, in_specs=in_specs, out_specs=out_specs, check_vma=False
    )
```

time: 121 us -> 133 us (1.099); the launches traced: 119 us -> 133 us
  Pallas kernels: 118 us -> 133 us
    pallas_call x1, Pallas kernels: 114 us -> 131 us  [per_device(): pl.pallas_call(functools.partial(gather_kernel, rows, cols, tile_rows, ti...]
    pallas_call x1, Pallas kernels: 4.57 us -> 2.02 us  [per_device(): pl.pallas_call(functools.partial(finish_kernel, part), out_shape=jax.Shap...]
where the time goes in v1:
time: 133 us
  Pallas kernels  133 us (100%)
    pallas_call x1, Pallas kernels, per_device(): pl.pallas_call(functools.partial(gather_kernel, rows, cols, tile_rows, ti...  131 us

profile of v1, /device:TPU:0, one launch (start us, length us, event | category | flops | bytes accessed | tf_op | source)
XLA Modules:
  0.0 132.9 jit_solution(183538948044580781)
XLA Ops:
  0.0 130.9 %gather.1 = (f32[16,512,128]{2,1,0:T(8,128)S(1)}, f32[16,128,512]{2,1,0:T(8,128)S(1)}, bf16[2,512,512]{2,1,0:T(8,128)(2,1)S(1)}) custom-call(f32[16,64,1024]{2,1,0:T(8,128)} %frames.1, s32[16,128]{1,0:T(8,128)} %class_in.1, s32[16,128]{1,0:T(8,128)} %mask_in.1, f32[8]{0:T(128)} %eff_in.1, f32[8]{0:T(128)} %cond_in.1), custom_call_target="tpu_custom_call" | custom-call | tf_op jit(solution)/shard_map/gather/pallas_call | solution.py:471
  130.9 2.0 %finish.1 = f32[16,128,512]{2,1,0:T(8,128)} custom-call(f32[16,512,128]{2,1,0:T(8,128)S(1)} %get-tuple-element.8.held, f32[16,128,512]{2,1,0:T(8,128)S(1)} %get-tuple-element.9.flux, bf16[2,512,512]{2,1,0:T(8,128)(2,1)S(1)} %get-tuple-element.10.mix_ref), custom_call_target="tpu_custom_call" | custom-call | tf_op jit(solution)/shard_map/finish/pallas_call | solution.py:503

commit v2 on v1

--- a/solution.py
+++ b/solution.py
@@ -11,6 +11,8 @@
 GROUP = 8
 LANES = 128
 STEPS = 8
+ROWS = 12
+LINES = 16
 VMEM_GATHER = 40 * 2**20
 MESH = pl.DeviceIdType.MESH
 
@@ -108,7 +110,7 @@
     part = tile_rows // steps
     source = row * cols + col
     mirror, pair = rows - 1 - row, lax.rem(row + mid, rows)
-    raw = ((row == mid - 1) | (row == mid)) & (lax.rem(col, 2) == 0)
+    raw = (row == mid - 1) | (row == mid)
 
     def wait_for(ref, sem):
         pltpu.make_async_copy(ref, ref, sem).wait()
@@ -234,71 +236,63 @@
     def spread(c, which, at):
         return coef[c, which, pl.ds(at, GROUP, stride=0), :]
 
-    def clear(side):
+    def relax(source_ref, side, begin, end, unroll, store):
+        base = side * half_rows - halo + PAD
+
+        @pl.loop(begin, end, step=unroll)
+        def _(i):
+            lines_at = [[source_ref[i + k, c] for c in range(cols)] for k in range(-1, unroll + 1)]
+            for k in range(unroll):
+                above, center, below = lines_at[k : k + 3]
+                ahead = [pltpu.roll(v, 1, 1) for v in center]
+                behind = [pltpu.roll(v, LANES - 1, 1) for v in center]
+                for c in range(cols):
+                    left = jnp.where(leftmost, ahead[c - 1] if c else nothing, ahead[c])
+                    right = jnp.where(rightmost, behind[c + 1] if c + 1 < cols else nothing, behind[c])
+                    laplace = below[c] + above[c] + right + left - 4.0 * center[c]
+                    store(i + k, c, center[c] + spread(c, 0, base + i + k) * laplace)
+
+    def keep(ref):
+        def store(i, c, value):
+            ref[i, c] = value
+        return store
+
+    def sweep(side, group, edge, store_last):
+        span = half_rows + 2 * halo
         for k in range(halo):
+            at = half_rows - halo * side + k
             for c in range(cols):
                 first[(half_rows + halo) * side + k, c] = nothing
-
-    def relax(source_ref, side, begin, end, store):
-        base = side * half_rows - halo + PAD
-
-        @pl.loop(begin, end)
-        def _(i):
-            center = [source_ref[i, c] for c in range(cols)]
-            ahead = [pltpu.roll(v, 1, 1) for v in center]
-            behind = [pltpu.roll(v, LANES - 1, 1) for v in center]
-            for c in range(cols):
-                left = jnp.where(leftmost, ahead[c - 1] if c else nothing, ahead[c])
-                right = jnp.where(rightmost, behind[c + 1] if c + 1 < cols else nothing, behind[c])
-                laplace = source_ref[i + 1, c] + source_ref[i - 1, c] + right + left - 4.0 * center[c]
-                store(i, c, center[c] + spread(c, 0, base + i) * laplace)
-
-    def passes(side, store_last):
-        def keep(ref):
-            def store(i, c, value):
-                ref[i, c] = value
-            return store
-
-        span = half_rows + 2 * halo
-        relax(first, side, 1, span - 1, keep(second))
-        relax(second, side, 2, span - 2, keep(first))
-        relax(first, side, halo, span - halo, store_last)
-
-    def sweep(side, group):
-        clear(side)
-
-        @pl.loop(0, half_rows + halo)
-        def _(k):
-            at = (half_rows - halo) * side + k
-            for c in range(cols):
-                first[halo * (1 - side) + k, c] = spread(c, 1, at + PAD) * line(c, group, at)
-
+                first[(half_rows + halo) * (1 - side) + k, c] = spread(c, 1, at + PAD) * edge(k, c, at)
+        for c in range(cols):
+            second[0, c] = nothing
+            second[span - 1, c] = nothing
+
+        @pl.loop(0, half_rows, step=LINES)
+        def _(j):
+            for k in range(LINES):
+                at = half_rows * side + j + k
+                for c in range(cols):
+                    first[halo + j + k, c] = spread(c, 1, at + PAD) * line(c, group, at)
+
+        relax(first, side, 1, span - 1, ROWS, keep(second))
+        relax(second, side, 1, span - 1, ROWS, keep(first))
+        relax(first, side, halo, span - halo, LINES, store_last)
+
+    def sweep_own(side, group):
         def store(i, c, value):
             j = i - halo
             at = pl.ds(aligned(group * GROUP, GROUP), GROUP)
             done[side * mid + j // tile_rows, c, lax.rem(j, tile_rows), at, :] = value
 
-        passes(side, store)
+        sweep(side, group, lambda k, c, at: line(c, group, at), store)
 
     def sweep_raw():
-        clear(half)
-
-        @pl.loop(0, half_rows)
-        def _(k):
-            at = half_rows * half + k
-            for c in range(cols):
-                first[halo + k, c] = spread(c, 1, at + PAD) * line(c, local // GROUP, at)
-
-        for k in range(halo):
-            for c in range(cols):
-                at = half_rows - halo * half + k
-                first[(half_rows + halo) * (1 - half) + k, c] = spread(c, 1, at + PAD) * edge_in[k, c]
-
         def store(i, c, value):
             j = i - halo
             done_far[j // tile_rows, c, lax.rem(j, tile_rows), :, :] = value
 
-        passes(half, store)
+        sweep(half, local // GROUP, lambda k, c, at: edge_in[k, c], store)
 
     groups = local // GROUP
 
@@ -325,7 +319,7 @@
 
     @pl.loop(0, groups)
     def _(g):
-        sweep(half, g)
+        sweep_own(half, g)
 
     own_slots = slots(source * local, local)
 
@@ -348,7 +342,7 @@
 
     @pl.loop(raw.astype(jnp.int32), groups)
     def _(g):
-        sweep(other, g)
+        sweep_own(other, g)
 
     def across(i):
         at = lax.rem(row * cols + col - half * (near + 1) + i, near + 1)
@@ -459,6 +453,7 @@
         rows % 2 == 0 and cols % 2 == 0 and local % (2 * GROUP) == 0 and tile_rows % PAD == 0
         and tile_rows % STEPS == 0 and tile_cols == LANES and total % (2 * LANES) == 0
         and near <= tile_rows and 2 * tile_rows <= total
+        and height // 2 % LINES == 0 and (height // 2 + 2 * PASSES - 2) % ROWS == 0
     )
     if not fits:
         return plain_device(frames, class_index, surface_mask, effusivity, conductivity)

time: 133 us -> 104 us (0.78)
  Pallas kernels: 133 us -> 104 us
    pallas_call x1, Pallas kernels: 131 us -> 102 us  [per_device(): pl.pallas_call(functools.partial(gather_kernel, rows, cols, tile_rows, ti...]
where the time goes in v2:
time: 104 us
  Pallas kernels  104 us (100%)
    pallas_call x1, Pallas kernels, per_device(): pl.pallas_call(functools.partial(gather_kernel, rows, cols, tile_rows, ti...  102 us

profile of v2, /device:TPU:0, one launch (start us, length us, event | category | flops | bytes accessed | tf_op | source)
XLA Modules:
  0.0 103.7 jit_solution(10595298787519628921)
XLA Ops:
  0.0 101.7 %gather.1 = (f32[16,512,128]{2,1,0:T(8,128)S(1)}, f32[16,128,512]{2,1,0:T(8,128)S(1)}, bf16[2,512,512]{2,1,0:T(8,128)(2,1)S(1)}) custom-call(f32[16,64,1024]{2,1,0:T(8,128)} %frames.1, s32[16,128]{1,0:T(8,128)} %class_in.1, s32[16,128]{1,0:T(8,128)} %mask_in.1, f32[8]{0:T(128)} %eff_in.1, f32[8]{0:T(128)} %cond_in.1), custom_call_target="tpu_custom_call" | custom-call | tf_op jit(solution)/shard_map/gather/pallas_call | solution.py:466
  101.7 2.0 %finish.1 = f32[16,128,512]{2,1,0:T(8,128)} custom-call(f32[16,512,128]{2,1,0:T(8,128)S(1)} %get-tuple-element.8.held, f32[16,128,512]{2,1,0:T(8,128)S(1)} %get-tuple-element.9.flux, bf16[2,512,512]{2,1,0:T(8,128)(2,1)S(1)} %get-tuple-element.10.mix_ref), custom_call_target="tpu_custom_call" | custom-call | tf_op jit(solution)/shard_map/finish/pallas_call | solution.py:498

commit v3 on v2

--- a/solution.py
+++ b/solution.py
@@ -10,7 +10,7 @@
 PAD = 8
 GROUP = 8
 LANES = 128
-STEPS = 8
+STEPS = 4
 ROWS = 12
 LINES = 16
 VMEM_GATHER = 40 * 2**20
@@ -110,7 +110,8 @@
     part = tile_rows // steps
     source = row * cols + col
     mirror, pair = rows - 1 - row, lax.rem(row + mid, rows)
-    raw = (row == mid - 1) | (row == mid)
+    inner = (row == mid - 1) | (row == mid)
+    raw = inner & (lax.rem(col, 2) == 0)
 
     def wait_for(ref, sem):
         pltpu.make_async_copy(ref, ref, sem).wait()
@@ -125,8 +126,7 @@
         )
 
     def in_half(i):
-        at = lax.rem(row * cols + col - half * (near + 1) + i, near + 1)
-        return half * mid + at // cols, lax.rem(at, cols)
+        return half * mid + lax.rem(row + i // cols, mid), lax.rem(col + i, cols)
 
     smalls = [
         pltpu.make_async_copy(src, dst, small_sem.at[i])
@@ -317,58 +317,63 @@
     wait_for(tiles(near), near_recv)
     wait_for(tiles(near), far_recv)
 
+    own_slots = slots(source * local, local)
+
+    def across(i):
+        return other * mid + lax.rem(row + i // cols, mid), lax.rem(col + i, cols)
+
+    def send_near(q):
+        pltpu.make_async_copy(
+            done.at[row, col, rows_of(q)], held.at[rows_of(q), own_slots], recv_sem.at[q]
+        ).start()
+
+        @pl.loop(1, near + 1)
+        def _(i):
+            to_row, to_col = in_half(i)
+            remote(
+                done.at[to_row, to_col, rows_of(q)], held.at[rows_of(q), own_slots],
+                near_send, recv_sem.at[q], to_row, to_col,
+            ).start()
+
+    def send_cross(q, skip):
+        count = local - skip
+
+        @pl.loop(0, near + 1)
+        def _(i):
+            to_row, to_col = across(i)
+            remote(
+                done.at[to_row, to_col, rows_of(q), pl.ds(skip, count)],
+                held.at[rows_of(q), slots(source * local + skip, count)],
+                cross_send, recv_sem.at[q], to_row, to_col,
+            ).start()
+
+    @pl.loop(raw.astype(jnp.int32), groups)
+    def _(g):
+        sweep_own(other, g)
+
+    @pl.when(raw)
+    def _():
+        @pl.loop(0, steps)
+        def _(q):
+            send_cross(q, GROUP)
+
+    @pl.when(inner & jnp.logical_not(raw))
+    def _():
+        @pl.loop(0, steps)
+        def _(q):
+            send_cross(q, 0)
+
     @pl.loop(0, groups)
     def _(g):
         sweep_own(half, g)
 
-    own_slots = slots(source * local, local)
-
-    def near_copy(q, i):
-        to_row, to_col = in_half(i)
-        return remote(
-            done.at[to_row, to_col, rows_of(q)], held.at[rows_of(q), own_slots],
-            near_send, recv_sem.at[q], to_row, to_col,
-        )
-
     @pl.loop(0, steps)
     def _(q):
-        pltpu.make_async_copy(
-            done.at[row, col, rows_of(q)], held.at[rows_of(q), own_slots], recv_sem.at[q]
-        ).start()
-
-        @pl.loop(1, near + 1)
-        def _(i):
-            near_copy(q, i).start()
-
-    @pl.loop(raw.astype(jnp.int32), groups)
-    def _(g):
-        sweep_own(other, g)
-
-    def across(i):
-        at = lax.rem(row * cols + col - half * (near + 1) + i, near + 1)
-        return other * mid + at // cols, lax.rem(at, cols)
-
-    def start_cross(skip):
-        count = local - skip
-
-        @pl.loop(0, steps)
-        def _(q):
-            @pl.loop(0, near + 1)
-            def _(i):
-                to_row, to_col = across(i)
-                remote(
-                    done.at[to_row, to_col, rows_of(q), pl.ds(skip, count)],
-                    held.at[rows_of(q), slots(source * local + skip, count)],
-                    cross_send, recv_sem.at[q], to_row, to_col,
-                ).start()
-
-    @pl.when(raw)
-    def _():
-        start_cross(GROUP)
-
-    @pl.when(jnp.logical_not(raw))
-    def _():
-        start_cross(0)
+        @pl.when(jnp.logical_not(inner))
+        def _():
+            send_cross(q, 0)
+
+        send_near(q)
 
     @pl.when(raw)
     def _():

time: 104 us -> 101 us (0.971)
  Pallas kernels: 104 us -> 100 us
    pallas_call x1, Pallas kernels: 102 us -> 98.1 us  [per_device(): pl.pallas_call(functools.partial(gather_kernel, rows, cols, tile_rows, ti...]
where the time goes in v3:
time: 101 us; the launch traced here: 100 us
  Pallas kernels  100 us (99%)
    pallas_call x1, Pallas kernels, per_device(): pl.pallas_call(functools.partial(gather_kernel, rows, cols, tile_rows, ti...  98.1 us
    pallas_call x1, Pallas kernels, per_device(): pl.pallas_call(functools.partial(finish_kernel, part), out_shape=jax.Shap...  2.02 us

profile of v3, /device:TPU:0, one launch (start us, length us, event | category | flops | bytes accessed | tf_op | source)
XLA Modules:
  0.0 100.1 jit_solution(17619018151012788742)
XLA Ops:
  0.0 98.1 %gather.1 = (f32[16,512,128]{2,1,0:T(8,128)S(1)}, f32[16,128,512]{2,1,0:T(8,128)S(1)}, bf16[2,512,512]{2,1,0:T(8,128)(2,1)S(1)}) custom-call(f32[16,64,1024]{2,1,0:T(8,128)} %frames.1, s32[16,128]{1,0:T(8,128)} %class_in.1, s32[16,128]{1,0:T(8,128)} %mask_in.1, f32[8]{0:T(128)} %eff_in.1, f32[8]{0:T(128)} %cond_in.1), custom_call_target="tpu_custom_call" | custom-call | tf_op jit(solution)/shard_map/gather/pallas_call | solution.py:471
  98.1 2.0 %finish.1 = f32[16,128,512]{2,1,0:T(8,128)} custom-call(f32[16,512,128]{2,1,0:T(8,128)S(1)} %get-tuple-element.8.held, f32[16,128,512]{2,1,0:T(8,128)S(1)} %get-tuple-element.9.flux, bf16[2,512,512]{2,1,0:T(8,128)(2,1)S(1)} %get-tuple-element.10.mix_ref), custom_call_target="tpu_custom_call" | custom-call | tf_op jit(solution)/shard_map/finish/pallas_call | solution.py:503

commit v4 on v3

--- a/solution.py
+++ b/solution.py
@@ -13,6 +13,7 @@
 STEPS = 4
 ROWS = 12
 LINES = 16
+EARLY = 1
 VMEM_GATHER = 40 * 2**20
 MESH = pl.DeviceIdType.MESH
 
@@ -97,7 +98,7 @@
     class_ref, mask_ref, eff_ref, cond_ref,
     load_sem, small_sem, coef_send, near_recv, pair_recv, far_recv,
     raw_send, raw_recv, edge_send, edge_recv,
-    near_send, cross_send, relay_send, recv_sem,
+    near_send, cross_send, relay_send, recv_sem, ready,
 ):
     row, col = lax.axis_index("row"), lax.axis_index("col")
     mid = rows // 2
@@ -128,6 +129,29 @@
     def in_half(i):
         return half * mid + lax.rem(row + i // cols, mid), lax.rem(col + i, cols)
 
+    barrier = pltpu.get_barrier_semaphore()
+
+    def greet(to_row, to_col):
+        pl.semaphore_signal(barrier, inc=1, device_id=(to_row, to_col), device_id_type=MESH)
+
+    def is_inner(at_row):
+        return (at_row == mid - 1) | (at_row == mid)
+
+    @pl.when(raw)
+    def _():
+        greet(mirror, col)
+
+    even = lax.rem(col, 2) == 0
+    greet(pair, col + (is_inner(pair) & even).astype(jnp.int32))
+
+    @pl.loop(1, near + 1)
+    def _(i):
+        to_row, to_col = in_half(i)
+
+        @pl.when(jnp.logical_not(is_inner(to_row) & (lax.rem(to_col, 2) == 0)))
+        def _():
+            greet(to_row, to_col)
+
     smalls = [
         pltpu.make_async_copy(src, dst, small_sem.at[i])
         for i, (src, dst) in enumerate(
@@ -141,17 +165,23 @@
             frames.at[:, :, c * LANES : (c + 1) * LANES], x.at[c, 0:local], load_sem
         ).start()
 
-    barrier = pltpu.get_barrier_semaphore()
-
-    @pl.when(raw)
-    def _():
-        pl.semaphore_signal(barrier, inc=1, device_id=(mirror, col), device_id_type=MESH)
-
-    pl.semaphore_signal(barrier, inc=1, device_id=(pair, col), device_id_type=MESH)
-
-    @pl.loop(1, near + 1)
-    def _(i):
-        pl.semaphore_signal(barrier, inc=1, device_id=in_half(i), device_id_type=MESH)
+    proxy = inner & jnp.logical_not(even)
+
+    far_rows = pl.ds(aligned(other * half_rows, PAD), half_rows)
+    near_rows = pl.ds(aligned(half * half_rows, PAD), half_rows)
+
+    def raw_copy(c):
+        return remote(
+            frames.at[0:GROUP, far_rows, c * LANES : (c + 1) * LANES],
+            x.at[c, local : local + GROUP, far_rows],
+            raw_send, raw_recv, mirror, col,
+        )
+
+    @pl.when(raw)
+    def _():
+        pl.semaphore_wait(barrier, 1)
+        for c in range(EARLY):
+            raw_copy(c).start()
 
     for copy in smalls:
         copy.wait()
@@ -174,7 +204,18 @@
             coef[c, k, 0:PAD] = jnp.zeros((PAD, LANES), jnp.float32)
             coef[c, k, PAD + height : 2 * PAD + height] = jnp.zeros((PAD, LANES), jnp.float32)
 
-    pl.semaphore_wait(barrier, near + 1 + raw.astype(jnp.int32))
+    @pl.when(jnp.logical_not(raw))
+    def _():
+        pl.semaphore_wait(barrier, near + 1 + proxy.astype(jnp.int32))
+
+    @pl.when(proxy)
+    def _():
+        pl.semaphore_signal(ready, inc=1, device_id=(row, col - 1), device_id_type=MESH)
+
+    @pl.when(raw)
+    def _():
+        pl.semaphore_wait(ready, 1)
+
 
     own_tile, pair_tile = tile_of(row, col), tile_of(pair, col)
     remote(own_tile, own_tile, coef_send.at[0], pair_recv, pair, col).start()
@@ -184,21 +225,11 @@
         to_row, to_col = in_half(i)
         remote(own_tile, own_tile, coef_send.at[1], near_recv, to_row, to_col).start()
 
-    far_rows = pl.ds(aligned(other * half_rows, PAD), half_rows)
-    near_rows = pl.ds(aligned(half * half_rows, PAD), half_rows)
-
-    def raw_copy(c):
-        return remote(
-            frames.at[0:GROUP, far_rows, c * LANES : (c + 1) * LANES],
-            x.at[c, local : local + GROUP, far_rows],
-            raw_send, raw_recv, mirror, col,
-        )
-
     edge_copy = remote(edge_out, edge_in, edge_send, edge_recv, mirror, col)
 
     @pl.when(raw)
     def _():
-        for c in range(cols):
+        for c in range(EARLY, cols):
             raw_copy(c).start()
 
     wait_for(x.at[:, 0:local], load_sem)
@@ -236,8 +267,7 @@
     def spread(c, which, at):
         return coef[c, which, pl.ds(at, GROUP, stride=0), :]
 
-    def relax(source_ref, side, begin, end, unroll, store):
-        base = side * half_rows - halo + PAD
+    def relax(source_ref, base, begin, end, unroll, store):
 
         @pl.loop(begin, end, step=unroll)
         def _(i):
@@ -259,6 +289,7 @@
 
     def sweep(side, group, edge, store_last):
         span = half_rows + 2 * halo
+        base = side * half_rows - halo + PAD
         for k in range(halo):
             at = half_rows - halo * side + k
             for c in range(cols):
@@ -275,9 +306,29 @@
                 for c in range(cols):
                     first[halo + j + k, c] = spread(c, 1, at + PAD) * line(c, group, at)
 
-        relax(first, side, 1, span - 1, ROWS, keep(second))
-        relax(second, side, 1, span - 1, ROWS, keep(first))
-        relax(first, side, halo, span - halo, LINES, store_last)
+        relax(first, base, 1, span - 1, ROWS, keep(second))
+        relax(second, base, 1, span - 1, ROWS, keep(first))
+        relax(first, base, halo, span - halo, LINES, store_last)
+
+    def sweep_tile(side, group, tile):
+        begin = side * half_rows + tile * tile_rows - halo
+        span = tile_rows + 2 * halo
+        for k in range(span):
+            at = begin + k
+            for c in range(cols):
+                first[k, c] = spread(c, 1, at + PAD) * line(c, group, lax.rem(at + height, height))
+        for c in range(cols):
+            second[0, c] = nothing
+            second[span - 1, c] = nothing
+
+        def store(i, c, value):
+            at = pl.ds(aligned(group * GROUP, GROUP), GROUP)
+            done[side * mid + tile, c, i - halo, at, :] = value
+
+        base = begin + PAD
+        relax(first, base, 1, span - 1, (span - 2) // 2, keep(second))
+        relax(second, base, 1, span - 1, (span - 2) // 2, keep(first))
+        relax(first, base, halo, span - halo, tile_rows, store)
 
     def sweep_own(side, group):
         def store(i, c, value):
@@ -335,33 +386,47 @@
                 near_send, recv_sem.at[q], to_row, to_col,
             ).start()
 
-    def send_cross(q, skip):
+    def cross_copy(q, skip, to_row, to_col):
         count = local - skip
-
+        return remote(
+            done.at[to_row, to_col, rows_of(q), pl.ds(skip, count)],
+            held.at[rows_of(q), slots(source * local + skip, count)],
+            cross_send, recv_sem.at[q], to_row, to_col,
+        )
+
+    def send_cross(q):
         @pl.loop(0, near + 1)
         def _(i):
-            to_row, to_col = across(i)
-            remote(
-                done.at[to_row, to_col, rows_of(q), pl.ds(skip, count)],
-                held.at[rows_of(q), slots(source * local + skip, count)],
-                cross_send, recv_sem.at[q], to_row, to_col,
-            ).start()
-
-    @pl.loop(raw.astype(jnp.int32), groups)
-    def _(g):
-        sweep_own(other, g)
-
-    @pl.when(raw)
+            cross_copy(q, 0, *across(i)).start()
+
+    @pl.when(raw)
+    def _():
+        @pl.loop(0, mid)
+        def _(t):
+            tile = lax.rem(row + t, mid)
+            to_row = other * mid + tile
+
+            @pl.loop(1, groups)
+            def _(g):
+                sweep_tile(other, g, tile)
+
+            @pl.loop(0, steps)
+            def _(q):
+                @pl.loop(0, cols)
+                def _(i):
+                    cross_copy(q, GROUP, to_row, lax.rem(col + i, cols)).start()
+
+    @pl.when(jnp.logical_not(raw))
+    def _():
+        @pl.loop(0, groups)
+        def _(g):
+            sweep_own(other, g)
+
+    @pl.when(inner & jnp.logical_not(raw))
     def _():
         @pl.loop(0, steps)
         def _(q):
-            send_cross(q, GROUP)
-
-    @pl.when(inner & jnp.logical_not(raw))
-    def _():
-        @pl.loop(0, steps)
-        def _(q):
-            send_cross(q, 0)
+            send_cross(q)
 
     @pl.loop(0, groups)
     def _(g):
@@ -371,7 +436,7 @@
     def _(q):
         @pl.when(jnp.logical_not(inner))
         def _():
-            send_cross(q, 0)
+            send_cross(q)
 
         send_near(q)
 
@@ -457,7 +522,7 @@
     fits = (
         rows % 2 == 0 and cols % 2 == 0 and local % (2 * GROUP) == 0 and tile_rows % PAD == 0
         and tile_rows % STEPS == 0 and tile_cols == LANES and total % (2 * LANES) == 0
-        and near <= tile_rows and 2 * tile_rows <= total
+        and near <= tile_rows and cols >= EARLY and 2 * tile_rows <= total
         and height // 2 % LINES == 0 and (height // 2 + 2 * PASSES - 2) % ROWS == 0
     )
     if not fits:
@@ -492,7 +557,7 @@
             pltpu.SMEM(conductivity.shape, f32),
             dma, dma((4,)), dma((3,)), dma, dma, dma,
             dma, dma, dma, dma,
-            dma, dma, dma, dma((STEPS,)),
+            dma, dma, dma, dma((STEPS,)), pltpu.SemaphoreType.REGULAR,
         ],
         compiler_params=pltpu.CompilerParams(
             collective_id=0, has_side_effects=True, vmem_limit_bytes=VMEM_GATHER

time: 101 us -> 98.9 us (0.979)
  Pallas kernels: 100 us -> 98.5 us
    pallas_call x1, Pallas kernels: 98.1 us -> 96.4 us  [per_device(): pl.pallas_call(functools.partial(gather_kernel, rows, cols, tile_rows, ti...]
where the time goes in v4:
time: 98.9 us; the launch traced here: 98.5 us
  Pallas kernels  98.5 us (100%)
    pallas_call x1, Pallas kernels, per_device(): pl.pallas_call(functools.partial(gather_kernel, rows, cols, tile_rows, ti...  96.4 us
    pallas_call x1, Pallas kernels, per_device(): pl.pallas_call(functools.partial(finish_kernel, part), out_shape=jax.Shap...  2.02 us

profile of v4, /device:TPU:0, one launch (start us, length us, event | category | flops | bytes accessed | tf_op | source)
XLA Modules:
  0.0 98.5 jit_solution(12845374807941649392)
XLA Ops:
  0.0 96.4 %gather.1 = (f32[16,512,128]{2,1,0:T(8,128)S(1)}, f32[16,128,512]{2,1,0:T(8,128)S(1)}, bf16[2,512,512]{2,1,0:T(8,128)(2,1)S(1)}) custom-call(f32[16,64,1024]{2,1,0:T(8,128)} %frames.1, s32[16,128]{1,0:T(8,128)} %class_in.1, s32[16,128]{1,0:T(8,128)} %mask_in.1, f32[8]{0:T(128)} %eff_in.1, f32[8]{0:T(128)} %cond_in.1), custom_call_target="tpu_custom_call" | custom-call | tf_op jit(solution)/shard_map/gather/pallas_call | solution.py:536
  96.5 2.0 %finish.1 = f32[16,128,512]{2,1,0:T(8,128)} custom-call(f32[16,512,128]{2,1,0:T(8,128)S(1)} %get-tuple-element.8.held, f32[16,128,512]{2,1,0:T(8,128)S(1)} %get-tuple-element.9.flux, bf16[2,512,512]{2,1,0:T(8,128)(2,1)S(1)} %get-tuple-element.10.mix_ref), custom_call_target="tpu_custom_call" | custom-call | tf_op jit(solution)/shard_map/finish/pallas_call | solution.py:568

commit v5 on v4

--- a/solution.py
+++ b/solution.py
@@ -126,6 +126,9 @@
             device_id=(to_row, to_col), device_id_type=MESH,
         )
 
+    def turn(i):
+        return lax.rem(col + lax.rem(i, cols // 2) * 2 + lax.rem(i // (cols // 2), 2), cols)
+
     def in_half(i):
         return half * mid + lax.rem(row + i // cols, mid), lax.rem(col + i, cols)
 
@@ -371,7 +374,7 @@
     own_slots = slots(source * local, local)
 
     def across(i):
-        return other * mid + lax.rem(row + i // cols, mid), lax.rem(col + i, cols)
+        return other * mid + lax.rem(row + i // cols, mid), turn(i)
 
     def send_near(q):
         pltpu.make_async_copy(
@@ -380,7 +383,7 @@
 
         @pl.loop(1, near + 1)
         def _(i):
-            to_row, to_col = in_half(i)
+            to_row, to_col = in_half(near + 1 - i)
             remote(
                 done.at[to_row, to_col, rows_of(q)], held.at[rows_of(q), own_slots],
                 near_send, recv_sem.at[q], to_row, to_col,
@@ -414,7 +417,7 @@
             def _(q):
                 @pl.loop(0, cols)
                 def _(i):
-                    cross_copy(q, GROUP, to_row, lax.rem(col + i, cols)).start()
+                    cross_copy(q, GROUP, to_row, turn(i)).start()
 
     @pl.when(jnp.logical_not(raw))
     def _():

time: 98.9 us -> 99 us (level)
  no operation moved by 1% of the time
where the time goes in v5:
time: 99 us; the launch traced here: 98.5 us
  Pallas kernels  98.5 us (99%)
    pallas_call x1, Pallas kernels, per_device(): pl.pallas_call(functools.partial(gather_kernel, rows, cols, tile_rows, ti...  96.5 us
    pallas_call x1, Pallas kernels, per_device(): pl.pallas_call(functools.partial(finish_kernel, part), out_shape=jax.Shap...  2.02 us

profile of v5, /device:TPU:0, one launch (start us, length us, event | category | flops | bytes accessed | tf_op | source)
XLA Modules:
  0.0 98.5 jit_solution(11421831144931859135)
XLA Ops:
  0.0 96.5 %gather.1 = (f32[16,512,128]{2,1,0:T(8,128)S(1)}, f32[16,128,512]{2,1,0:T(8,128)S(1)}, bf16[2,512,512]{2,1,0:T(8,128)(2,1)S(1)}) custom-call(f32[16,64,1024]{2,1,0:T(8,128)} %frames.1, s32[16,128]{1,0:T(8,128)} %class_in.1, s32[16,128]{1,0:T(8,128)} %mask_in.1, f32[8]{0:T(128)} %eff_in.1, f32[8]{0:T(128)} %cond_in.1), custom_call_target="tpu_custom_call" | custom-call | tf_op jit(solution)/shard_map/gather/pallas_call | solution.py:539
  96.5 2.0 %finish.1 = f32[16,128,512]{2,1,0:T(8,128)} custom-call(f32[16,512,128]{2,1,0:T(8,128)S(1)} %get-tuple-element.8.held, f32[16,128,512]{2,1,0:T(8,128)S(1)} %get-tuple-element.9.flux, bf16[2,512,512]{2,1,0:T(8,128)(2,1)S(1)} %get-tuple-element.10.mix_ref), custom_call_target="tpu_custom_call" | custom-call | tf_op jit(solution)/shard_map/finish/pallas_call | solution.py:571

commit v6 on v5

--- a/solution.py
+++ b/solution.py
@@ -236,7 +236,7 @@
             raw_copy(c).start()
 
     wait_for(x.at[:, 0:local], load_sem)
-    lines = x.reshape(cols, (local + GROUP) * height, LANES)
+    lines = x.reshape(cols, x.shape[1] * height, LANES)
 
     def line(c, group, at):
         return lines[c, pl.ds(group * (GROUP * height) + at, GROUP, stride=height), :]
@@ -546,8 +546,8 @@
         in_specs=[hbm] * 5,
         out_specs=(vmem, vmem, vmem),
         scratch_shapes=[
-            pltpu.VMEM((cols, local + GROUP, height, LANES), f32),
-            pltpu.VMEM((cols, 2, height + 2 * PAD, LANES), f32),
+            pltpu.VMEM((cols, local + 2 * GROUP, height, LANES), f32),
+            pltpu.VMEM((cols, 2, height + 3 * PAD, LANES), f32),
             pltpu.VMEM((rows, cols, tile_rows, local, LANES), f32),
             pltpu.VMEM((rows // 2, cols, tile_rows, GROUP, LANES), f32),
             pltpu.VMEM((span, cols, GROUP, LANES), f32),

time: 99 us -> 98.9 us (level)
  no operation moved by 1% of the time
where the time goes in v6:
time: 98.9 us; the launch traced here: 98.5 us
  Pallas kernels  98.5 us (100%)
    pallas_call x1, Pallas kernels, per_device(): pl.pallas_call(functools.partial(gather_kernel, rows, cols, tile_rows, ti...  96.4 us
    pallas_call x1, Pallas kernels, per_device(): pl.pallas_call(functools.partial(finish_kernel, part), out_shape=jax.Shap...  2.02 us

profile of v6, /device:TPU:0, one launch (start us, length us, event | category | flops | bytes accessed | tf_op | source)
XLA Modules:
  0.0 98.5 jit_solution(16892290182473369413)
XLA Ops:
  0.0 96.4 %gather.1 = (f32[16,512,128]{2,1,0:T(8,128)S(1)}, f32[16,128,512]{2,1,0:T(8,128)S(1)}, bf16[2,512,512]{2,1,0:T(8,128)(2,1)S(1)}) custom-call(f32[16,64,1024]{2,1,0:T(8,128)} %frames.1, s32[16,128]{1,0:T(8,128)} %class_in.1, s32[16,128]{1,0:T(8,128)} %mask_in.1, f32[8]{0:T(128)} %eff_in.1, f32[8]{0:T(128)} %cond_in.1), custom_call_target="tpu_custom_call" | custom-call | tf_op jit(solution)/shard_map/gather/pallas_call | solution.py:539
  96.5 2.0 %finish.1 = f32[16,128,512]{2,1,0:T(8,128)} custom-call(f32[16,512,128]{2,1,0:T(8,128)S(1)} %get-tuple-element.8.held, f32[16,128,512]{2,1,0:T(8,128)S(1)} %get-tuple-element.9.flux, bf16[2,512,512]{2,1,0:T(8,128)(2,1)S(1)} %get-tuple-element.10.mix_ref), custom_call_target="tpu_custom_call" | custom-call | tf_op jit(solution)/shard_map/finish/pallas_call | solution.py:571

commit v7 on v6

--- a/solution.py
+++ b/solution.py
@@ -431,13 +431,17 @@
         def _(q):
             send_cross(q)
 
+    @pl.when(jnp.logical_not(inner))
+    def _():
+        send_cross(0)
+
     @pl.loop(0, groups)
     def _(g):
         sweep_own(half, g)
 
     @pl.loop(0, steps)
     def _(q):
-        @pl.when(jnp.logical_not(inner))
+        @pl.when(jnp.logical_not(inner) & (q > 0))
         def _():
             send_cross(q)
 

time: 98.9 us -> 99 us (level)
  no operation moved by 1% of the time
where the time goes in v7:
time: 99 us; the launch traced here: 98.6 us
  Pallas kernels  98.6 us (100%)
    pallas_call x1, Pallas kernels, per_device(): pl.pallas_call(functools.partial(gather_kernel, rows, cols, tile_rows, ti...  96.5 us
    pallas_call x1, Pallas kernels, per_device(): pl.pallas_call(functools.partial(finish_kernel, part), out_shape=jax.Shap...  2.02 us

profile of v7, /device:TPU:0, one launch (start us, length us, event | category | flops | bytes accessed | tf_op | source)
XLA Modules:
  0.0 98.6 jit_solution(14912687058389538612)
XLA Ops:
  0.0 96.5 %gather.1 = (f32[16,512,128]{2,1,0:T(8,128)S(1)}, f32[16,128,512]{2,1,0:T(8,128)S(1)}, bf16[2,512,512]{2,1,0:T(8,128)(2,1)S(1)}) custom-call(f32[16,64,1024]{2,1,0:T(8,128)} %frames.1, s32[16,128]{1,0:T(8,128)} %class_in.1, s32[16,128]{1,0:T(8,128)} %mask_in.1, f32[8]{0:T(128)} %eff_in.1, f32[8]{0:T(128)} %cond_in.1), custom_call_target="tpu_custom_call" | custom-call | tf_op jit(solution)/shard_map/gather/pallas_call | solution.py:543
  96.5 2.0 %finish.1 = f32[16,128,512]{2,1,0:T(8,128)} custom-call(f32[16,512,128]{2,1,0:T(8,128)S(1)} %get-tuple-element.8.held, f32[16,128,512]{2,1,0:T(8,128)S(1)} %get-tuple-element.9.flux, bf16[2,512,512]{2,1,0:T(8,128)(2,1)S(1)} %get-tuple-element.10.mix_ref), custom_call_target="tpu_custom_call" | custom-call | tf_op jit(solution)/shard_map/finish/pallas_call | solution.py:575
